TPU v7x, 32 devices: a whole 2x2x4 slice. The times are simulated.
32 devices in a mesh: kpt: 4 (over y, core), row: 4 (over z), col: 2 (over x).
Axes of the slice: x: 2, y: 2, z: 4, core: 2. Of those that a mesh axis runs over, the one named last changes fastest.
Arguments:
- a_matrix: bfloat16 [8, 4096, 4096], P('kpt', 'row', 'col'), parts along dimension 0, may hold values from -6 to 6
- b_matrix: bfloat16 [8, 4096, 4096], P('kpt', 'row', 'col'), parts along dimension 0, may hold values from -0.09375 to 0.09375
- a_level: int32 [128, 32], P('kpt'), parts along dimension 0, may hold values from 0 to 4, as said below
- b_level: int32 [128, 32], P('kpt'), parts along dimension 0, may hold values from 0 to 4, as said below
- limit: int32 [128, 32], P(('kpt', 'row'), 'col'), parts along dimension 0, may hold values from 3 to 8
Outputs:
- product: bfloat16 [8, 4096, 4096], P('kpt', 'row', 'col'), parts along dimension 0
- kept_count: int32 [128, 32], P(('kpt', 'row'), 'col'), parts along dimension 0
- kept_total: int32 [4], P('kpt'), parts along dimension 0
There are 4 independent parts, one for each index of `kpt`. A program takes and returns all parts, laid end to end along the dimension named above; each array names one. Nothing has to cross between parts.
Inputs may be any that keep to these rules, and one draw needn't show every extreme that they name: Each block's level is 0 (empty) or its norm exponent 1 to 4; the share of occupied blocks rises from some a sixth in the first block row of a_level (block column of b_level) to some six in seven in the last. `b_level`: as for a_level, with the share rising along block columns.
All inputs are finite; a program needn't handle non-finite values.
Results may differ from a plain program's by a relative error of at most 0.001.
Values may be sent and summed in bfloat16 or wider, within the bound.
No kernel may reach another device: no remote copies, remote signals or barrier semaphores. Data moves between devices by JAX's collectives and lax.ppermute only.
A program may use at most 576 MiB of HBM per device.

v0:
```python
import jax
import jax.numpy as jnp
from jax import lax
from jax.sharding import PartitionSpec as P

BLK = 128


def level_scale(levels):
    power = jnp.power(jnp.float32(2.0), (1 - levels).astype(jnp.float32))
    return jnp.where(levels > 0, power, jnp.float32(0.0))


def spread_blocks(small):
    return jnp.repeat(jnp.repeat(small, BLK, axis=0), BLK, axis=1)


def block_terms(a_piece, a_lev, b_piece, b_lev, limit):
    keep = (
        (a_lev[:, :, None] > 0)
        & (b_lev[None, :, :] > 0)
        & (a_lev[:, :, None] + b_lev[None, :, :] <= limit[:, None, :])
    )
    counted = jnp.sum(keep.astype(jnp.int32), axis=1)
    results = []
    for column in range(limit.shape[1]):
        mask = jnp.repeat(keep[:, :, column], BLK, axis=0)
        masked = jnp.where(mask[None], a_piece, jnp.zeros((), jnp.bfloat16))
        right = b_piece[:, :, column * BLK : (column + 1) * BLK]
        real_real = jnp.dot(masked[0], right[0], preferred_element_type=jnp.float32)
        imag_imag = jnp.dot(masked[1], right[1], preferred_element_type=jnp.float32)
        real_imag = jnp.dot(masked[0], right[1], preferred_element_type=jnp.float32)
        imag_real = jnp.dot(masked[1], right[0], preferred_element_type=jnp.float32)
        results.append(jnp.stack([real_real - imag_imag, real_imag + imag_real]))
    return (jnp.concatenate(results, axis=2), counted)


def shards(a_matrix, b_matrix, a_level, b_level, limit):
    row_place = lax.axis_index("row")
    col_place = lax.axis_index("col")
    row_blocks = a_matrix.shape[1] // BLK
    col_blocks = a_matrix.shape[2] // BLK
    a_own = lax.dynamic_slice(
        a_level, (row_place * row_blocks, col_place * col_blocks), (row_blocks, col_blocks)
    )
    b_own = lax.dynamic_slice(
        b_level, (row_place * row_blocks, col_place * col_blocks), (row_blocks, col_blocks)
    )
    a_eff = a_matrix * spread_blocks(level_scale(a_own)).astype(jnp.bfloat16)[None]
    b_eff = b_matrix * spread_blocks(level_scale(b_own)).astype(jnp.bfloat16)[None]
    a_band = lax.dynamic_slice_in_dim(a_level, row_place * row_blocks, row_blocks, 0)
    b_band = lax.dynamic_slice_in_dim(b_level, col_place * col_blocks, col_blocks, 1)
    a_levels = jnp.repeat(a_band, BLK, axis=1)
    b_levels = jnp.repeat(b_band, BLK, axis=0)
    a_whole = lax.all_gather(a_eff, "col", axis=2, tiled=True)
    added, counted = block_terms(
        a_whole, a_levels, lax.all_gather(b_eff, "row", axis=1, tiled=True), b_levels, limit
    )
    kept_count = counted // BLK
    kept_total = lax.psum(jnp.sum(kept_count).reshape(1), ("row", "col"))
    return (added.astype(jnp.bfloat16), kept_count, kept_total)


def solution(mesh):
    in_specs = (
        P("kpt", "row", "col"),
        P("kpt", "row", "col"),
        P("kpt", None),
        P("kpt", None),
        P(("kpt", "row"), "col"),
    )
    out_specs = (P("kpt", "row", "col"), P(("kpt", "row"), "col"), P("kpt"))
    return jax.shard_map(shards, mesh=mesh, in_specs=in_specs, out_specs=out_specs, check_vma=False)
```

profile of v0, /device:TPU:0, one launch (start us, length us, event | category | flops | bytes accessed | tf_op | source)
XLA Modules:
  0.0 1229.6 jit_solution(12622931891409190300)
XLA Ops:
  25.3 8.4 broadcast_multiply_fusion
  37.7 14.6 %psum.7 = s32[1]{0:T(128)} all-reduce(s32[1]{0:T(128)} %bitcast.131), channel_id=1, replica_groups=mesh['kpt'=4,'row'=4,'col'=2] {'row','col'}, use_global_device_ids=true, to_apply=%region_2.3 | all-reduce | flops 1 | bytes 8 | tf_op jit(solution)/shard_map/psum | solution.py:60
  52.3 168.1 %all-gather.3.cloned.1.call-done = bf16[2,1024,4096]{2,1,0:T(8,128)(2,1)} async-done(((bf16[2,1024,2048]{2,1,0:T(8,128)(2,1)}), bf16[2,1024,4096]{2,1,0:T(8,128)(2,1)}) %all-gather.3.cloned.1.call-update) | async-done | bytes 16777232 | tf_op jit(solution)/shard_map/all_gather | solution.py:55
  285.2 115.4 %broadcast_select_fusion = (bf16[2,1024,4096]{2,1,0:T(8,128)(2,1)}, bf16[2,1024,4096]{2,1,0:T(8,128)(2,1)}, bf16[2,1024,4096]{2,1,0:T(8,128)(2,1)}, bf16[2,1024,...) fusion(bf16[2,1024,4096]{2,1,0:T(8,128)(2,1)} %all-gather.3.clo, ...), kind=kLoop, calls=%fused_computation | loop fusion | flops 134217728 | bytes 352321536 | tf_op jit(solution)/shard_map/jit(_where)/select_n | solution.py:28
  400.6 382.8 %all-gather.5.cloned.1.call-done = bf16[2,4096,2048]{2,1,0:T(8,128)(2,1)} async-done(((bf16[2,1024,2048]{2,1,0:T(8,128)(2,1)}), bf16[2,4096,2048]{2,1,0:T(8,128)(2,1)}) %all-gather.5.cloned.1.call-update) | async-done | bytes 33554448 | tf_op jit(solution)/shard_map/all_gather | solution.py:57
  783.4 6.7 fusion.1
  811.6 6.5 fusion.4
  818.1 6.7 fusion.157
  838.6 6.5 fusion.8
  859.0 6.7 fusion.13
  865.8 6.5 fusion.12
  872.3 6.5 fusion.153
  892.6 6.5 fusion.16
  899.2 6.9 fusion.151
  919.9 6.5 fusion.20
  926.5 6.5 fusion.149
  940.3 6.7 fusion.25
  953.5 6.5 fusion.147
  973.9 6.5 fusion.28
  980.4 6.7 fusion.145
  1001.0 6.5 fusion.32
  1007.5 6.5 fusion.143
  1021.3 6.9 fusion.37
  1055.1 6.5 fusion.40
  1061.7 6.7 fusion.139
  1082.2 6.5 fusion.44
  1102.6 6.7 fusion.49
  1136.2 6.5 fusion.52
  1142.7 6.9 fusion.133
  1163.4 6.5 fusion.56
  1190.3 6.7 fusion.60
  1210.9 11.6 copy.28
  (104 shorter events, 342.0 us)
Async XLA Ops:
  7.2 213.3 %all-gather.3.cloned.1.call-start = ((), (), s32[]{:S(2)}) async-start(), calls=%async_computation | async-start | bytes 25165824 | tf_op jit(solution)/shard_map/all_gather | solution.py:55
  7.2 7.6 copy-start.1
  18.6 764.8 %all-gather.5.cloned.1.call-start = ((), (), s32[]{:S(2)}) async-start(), calls=%async_computation.1 | async-start | bytes 41943040 | tf_op jit(solution)/shard_map/all_gather | solution.py:57
  25.3 8.4 copy-start.2
  25.3 9.6 copy-start.3
  783.4 8.5 copy-start
Sparse Core Ops, SparseCore 0:
  18.7 201.6 all-gather.2
  222.0 561.3 all-gather.4
where the time goes:
time: 1240 us; the launch traced here: 1230 us
  waiting for transfers between devices  551 us (44%)
  matrix products  412 us (33%)
  other arithmetic  144 us (12%)
  local copies, waits for them, and re-layouts  92.9 us (7%)
  between operations  14.8 us (1%)
  blocking collectives  14.6 us (1%)
    all_gather x1, waiting for transfers between devices, shards(): lax.all_gather(b_eff, 'row', axis=1, tiled=True)  383 us
    all_gather x1, waiting for transfers between devices, shards(): a_whole = lax.all_gather(a_eff, 'col', axis=2, tiled=True)  168 us
    select_n x1, other arithmetic, block_terms(): masked = jnp.where(mask[None], a_piece, jnp.zeros((), jnp.bfloat16))  115 us
    dot_general x16, matrix products, block_terms(): real_real = jnp.dot(masked[0], right[0], preferred_element_type=jnp.float32)  105 us
    dot_general x16, matrix products, block_terms(): imag_imag = jnp.dot(masked[1], right[1], preferred_element_type=jnp.float32)  103 us
    dot_general x16, matrix products, block_terms(): real_imag = jnp.dot(masked[0], right[1], preferred_element_type=jnp.float32)  102 us
    dot_general x16, matrix products, block_terms(): imag_real = jnp.dot(masked[1], right[0], preferred_element_type=jnp.float32)  102 us
    broadcast_in_dim x16, local copies, waits for them, and re-layouts, block_terms(): mask = jnp.repeat(keep[:, :, column], BLK, axis=0)  64.8 us
  transfers between devices with their start and end apart: 2, of which 2 were waited for; matrix products, arithmetic and copies ran while one was open for 16% of the time, Pallas kernels for 0%

commit v1 on v0

--- a/solution.py
+++ b/solution.py
@@ -52,7 +52,14 @@
     b_band = lax.dynamic_slice_in_dim(b_level, col_place * col_blocks, col_blocks, 1)
     a_levels = jnp.repeat(a_band, BLK, axis=1)
     b_levels = jnp.repeat(b_band, BLK, axis=0)
-    a_whole = lax.all_gather(a_eff, "col", axis=2, tiled=True)
+    ways, here = (lax.axis_size("col"), lax.axis_index("col"))
+    a_whole, reach = (a_eff, 1)
+    while reach < ways:
+        theirs = lax.ppermute(a_whole, "col", [(d, d ^ reach) for d in range(ways)])
+        mine_first = jnp.concatenate([a_whole, theirs], axis=2)
+        theirs_first = jnp.concatenate([theirs, a_whole], axis=2)
+        a_whole = jnp.where(here & reach == 0, mine_first, theirs_first)
+        reach = 2 * reach
     added, counted = block_terms(
         a_whole, a_levels, lax.all_gather(b_eff, "row", axis=1, tiled=True), b_levels, limit
     )

time: 1240 us -> 951 us (0.77)
  waiting for transfers between devices: 551 us -> 129 us
  blocking collectives: 14.6 us -> 205 us
  matrix products: 412 us -> 326 us
  other arithmetic: 144 us -> 205 us
  local copies, waits for them, and re-layouts: 92.9 us -> 58.1 us
    all_gather x1, waiting for transfers between devices: 383 us -> 129 us  [shards(): lax.all_gather(b_eff, 'row', axis=1, tiled=True)]
    psum x1, blocking collectives: 14.6 us -> 205 us  [shards(): kept_total = lax.psum(jnp.sum(kept_count).reshape(1), ('row', 'col'))]
    all_gather x1 -> x0, waiting for transfers between devices: 168 us -> none  [shards(): a_whole = lax.all_gather(a_eff, 'col', axis=2, tiled=True)]
    select_n x1 -> x6, other arithmetic: 115 us -> 176 us  [block_terms(): masked = jnp.where(mask[None], a_piece, jnp.zeros((), jnp.bfloat16))]
    dot_general x16, matrix products: 103 us -> 68.5 us  [block_terms(): imag_imag = jnp.dot(masked[1], right[1], preferred_element_type=jnp.float32)]
    broadcast_in_dim x16, local copies, waits for them, and re-layouts: 64.8 us -> 31.5 us  [block_terms(): mask = jnp.repeat(keep[:, :, column], BLK, axis=0)]
    dot_general x16, matrix products: 102 us -> 80.7 us  [block_terms(): real_imag = jnp.dot(masked[0], right[1], preferred_element_type=jnp.float32)]
    dot_general x16, matrix products: 102 us -> 84.5 us  [block_terms(): imag_real = jnp.dot(masked[1], right[0], preferred_element_type=jnp.float32)]
  transfers between devices with their start and end apart: 2 -> 2, of which waited for: 2 -> 1; matrix products, arithmetic and copies ran while one was open for 16% -> 24% of each run, Pallas kernels for 0% -> 0%
where the time goes in v1:
time: 951 us; the launch traced here: 942 us
  matrix products  326 us (34%)
  other arithmetic  205 us (22%)
  blocking collectives  205 us (22%)
  waiting for transfers between devices  129 us (14%)
  local copies, waits for them, and re-layouts  58.1 us (6%)
  between operations  15.7 us (2%)
    psum x1, blocking collectives, shards(): kept_total = lax.psum(jnp.sum(kept_count).reshape(1), ('row', 'col'))  205 us
    select_n x6, other arithmetic, block_terms(): masked = jnp.where(mask[None], a_piece, jnp.zeros((), jnp.bfloat16))  176 us
    all_gather x1, waiting for transfers between devices, shards(): lax.all_gather(b_eff, 'row', axis=1, tiled=True)  129 us
    dot_general x16, matrix products, block_terms(): real_real = jnp.dot(masked[0], right[0], preferred_element_type=jnp.float32)  92.2 us
    dot_general x16, matrix products, block_terms(): imag_real = jnp.dot(masked[1], right[0], preferred_element_type=jnp.float32)  84.5 us
    dot_general x16, matrix products, block_terms(): real_imag = jnp.dot(masked[0], right[1], preferred_element_type=jnp.float32)  80.7 us
    dot_general x16, matrix products, block_terms(): imag_imag = jnp.dot(masked[1], right[1], preferred_element_type=jnp.float32)  68.5 us
    broadcast_in_dim x16, local copies, waits for them, and re-layouts, block_terms(): mask = jnp.repeat(keep[:, :, column], BLK, axis=0)  31.5 us
  transfers between devices with their start and end apart: 2, of which 1 were waited for; matrix products, arithmetic and copies ran while one was open for 24% of the time, Pallas kernels for 0%

profile of v1, /device:TPU:0, one launch (start us, length us, event | category | flops | bytes accessed | tf_op | source)
XLA Modules:
  0.0 942.4 jit_solution(15675251617840426544)
XLA Ops:
  25.3 8.5 broadcast_multiply_fusion.1
  40.7 205.5 %psum.7 = s32[1]{0:T(128)} all-reduce(s32[1]{0:T(128)} %bitcast.131), channel_id=1, replica_groups=mesh['kpt'=4,'row'=4,'col'=2] {'row','col'}, use_global_device_ids=true, to_apply=%region_2.3 | all-reduce | flops 1 | bytes 8 | tf_op jit(solution)/shard_map/psum | solution.py:67
  248.2 20.4 %broadcast_select_fusion.15 = bf16[2,1024,4096]{2,1,0:T(8,128)(2,1)} fusion(pred[1024,4096]{1,0:T(8,128)(4,1)S(1)} %bitcast.601, bf16[2,1024,2048]{2,1,0:T(8,128)(2,1)} %broadcast_multiply_fusion.1, bf16[2,1024,2048]{2,1,0:T(8,128)(2,1)} %collective-permute-done, pred[]{:T(512)S(6)} %eq.3), kind=kLoop, calls=%fused_computation.16 | loop fusion | flops 83886080 | bytes 37748736 | tf_op jit(solution)/shard_map/jit(_where)/select_n | solution.py:28
  274.5 31.1 %broadcast_select_fusion.4 = (bf16[2,1024,4096]{2,1,0:T(8,128)(2,1)}, bf16[2,1024,4096]{2,1,0:T(8,128)(2,1)}, bf16[2,1024,4096]{2,1,0:T(8,128)(2,1)}) fusion(pred[1024,4096]{1,0:T(8,128)(4,1)S(1)} %bitcast.587, bf16[2,1024,2048]{2,1,0:T(8,128)(2,1)} %broadcast_multiply_fusion.1, bf16[2,1024,2048]{2,1,0:T(8,128)(2,1)} %collective-permute-done, pred[]{:T(512)S(6)} %eq.3, ...), kind=kLoop, calls=%fused_computation.5 | loop fusion | flops 100663296 | bytes 79691776 | tf_op jit(solution)/shard_map/jit(_where)/select_n | solution.py:28
  311.5 31.3 %broadcast_select_fusion.3 = (bf16[2,1024,4096]{2,1,0:T(8,128)(2,1)}, bf16[2,1024,4096]{2,1,0:T(8,128)(2,1)}, bf16[2,1024,4096]{2,1,0:T(8,128)(2,1)}) fusion(pred[1024,4096]{1,0:T(8,128)(4,1)S(1)} %bitcast.588, bf16[2,1024,2048]{2,1,0:T(8,128)(2,1)} %broadcast_multiply_fusion.1, bf16[2,1024,2048]{2,1,0:T(8,128)(2,1)} %collective-permute-done, pred[]{:T(512)S(6)} %eq.3, ...), kind=kLoop, calls=%fused_computation.4 | loop fusion | flops 100663296 | bytes 79691776 | tf_op jit(solution)/shard_map/jit(_where)/select_n | solution.py:28
  348.8 31.1 %broadcast_select_fusion.2 = (bf16[2,1024,4096]{2,1,0:T(8,128)(2,1)}, bf16[2,1024,4096]{2,1,0:T(8,128)(2,1)}, bf16[2,1024,4096]{2,1,0:T(8,128)(2,1)}) fusion(pred[1024,4096]{1,0:T(8,128)(4,1)S(1)} %bitcast.589, bf16[2,1024,2048]{2,1,0:T(8,128)(2,1)} %broadcast_multiply_fusion.1, bf16[2,1024,2048]{2,1,0:T(8,128)(2,1)} %collective-permute-done, pred[]{:T(512)S(6)} %eq.3, ...), kind=kLoop, calls=%fused_computation.3 | loop fusion | flops 100663296 | bytes 79691776 | tf_op jit(solution)/shard_map/jit(_where)/select_n | solution.py:28
  385.7 31.1 %broadcast_select_fusion.1 = (bf16[2,1024,4096]{2,1,0:T(8,128)(2,1)}, bf16[2,1024,4096]{2,1,0:T(8,128)(2,1)}, bf16[2,1024,4096]{2,1,0:T(8,128)(2,1)}) fusion(pred[1024,4096]{1,0:T(8,128)(4,1)S(1)} %bitcast.590, bf16[2,1024,2048]{2,1,0:T(8,128)(2,1)} %broadcast_multiply_fusion.1, bf16[2,1024,2048]{2,1,0:T(8,128)(2,1)} %collective-permute-done, pred[]{:T(512)S(6)} %eq.3, ...), kind=kLoop, calls=%fused_computation.2 | loop fusion | flops 100663296 | bytes 79691776 | tf_op jit(solution)/shard_map/jit(_where)/select_n | solution.py:28
  422.7 31.4 %broadcast_select_fusion = (bf16[2,1024,4096]{2,1,0:T(8,128)(2,1)}, bf16[2,1024,4096]{2,1,0:T(8,128)(2,1)}, bf16[2,1024,4096]{2,1,0:T(8,128)(2,1)}) fusion(pred[1024,4096]{1,0:T(8,128)(4,1)S(1)} %bitcast.584, bf16[2,1024,2048]{2,1,0:T(8,128)(2,1)} %broadcast_multiply_fusion.1, bf16[2,1024,2048]{2,1,0:T(8,128)(2,1)} %collective-permute-done, pred[]{:T(512)S(6)} %eq.3, ...), kind=kLoop, calls=%fused_computation.1 | loop fusion | flops 100663296 | bytes 79691776 | tf_op jit(solution)/shard_map/jit(_where)/select_n | solution.py:28
  454.1 128.9 %all-gather.2.cloned.1.call-done = bf16[2,4096,2048]{2,1,0:T(8,128)(2,1)} async-done(((bf16[2,1024,2048]{2,1,0:T(8,128)(2,1)}), bf16[2,4096,2048]{2,1,0:T(8,128)(2,1)}) %all-gather.2.cloned.1.call-update) | async-done | bytes 33554448 | tf_op jit(solution)/shard_map/all_gather | solution.py:64
  583.1 6.7 fusion.2
  589.7 6.7 fusion.3
  605.7 7.1 fusion.6
  617.0 6.8 fusion.158
  623.9 6.7 fusion.157
  644.0 6.8 fusion.155
  660.0 6.7 fusion.154
  666.7 6.7 fusion.153
  687.2 6.7 fusion.151
  703.0 6.7 fusion.150
  709.7 6.7 fusion.149
  729.9 6.7 fusion.147
  745.7 6.9 fusion.146
  752.6 6.7 fusion.145
  772.7 6.7 fusion.143
  788.9 6.7 fusion.142
  795.6 6.7 fusion.141
  815.9 6.7 fusion.139
  841.0 7.3 fusion.50
  861.8 7.1 fusion.54
  882.7 7.1 fusion.58
  903.3 7.3 fusion.62
  923.8 11.6 %copy.28 = bf16[2,1024,2048]{2,1,0:T(8,128)(2,1)} copy(bf16[2,1024,2048]{1,2,0:T(8,128)(2,1)} %maximum_dynamic-update-slice_fusion) | data formatting | bytes 16777216
  (250 shorter events, 246.4 us)
Async XLA Ops:
  7.2 575.9 %all-gather.2.cloned.1.call-start = ((), (), s32[]{:S(2)}) async-start(), calls=%async_computation | async-start | bytes 41943040 | tf_op jit(solution)/shard_map/all_gather | solution.py:64
  18.7 18.1 %copy-start.2 = (s32[8,16]{1,0:T(8,128)S(1)}, s32[8,16]{1,0:T(8,128)}, u32[]{:S(2)}) copy-start(s32[8,16]{1,0:T(8,128)} %param.9) | copy-start | bytes 1540
  18.7 18.9 %copy-start.1 = (s32[32,32]{1,0:T(8,128)S(1)}, s32[32,32]{1,0:T(8,128)}, u32[]{:S(2)}) copy-start(s32[32,32]{1,0:T(8,128)} %param.8) | copy-start | bytes 12292
  33.8 212.4 %collective-permute-start = (bf16[2,1024,2048]{2,1,0:T(8,128)(2,1)}, bf16[2,1024,2048]{2,1,0:T(8,128)(2,1)}, u32[]{:S(2)}, u32[]{:S(2)}) collective-permute-start(bf16[2,1024,2048]{2,1,0:T(8,128)(2,1)} %broadcast_multiply_fusion.1), channel_id=1, source_target_pairs={{0,1},{1,0},{2,3},{3,2},{4,5},{5,4},{6,7},{7,6},{8,9},{9,8},{10,11... | collective-permute-start | bytes 25165832 | tf_op jit(solution)/shard_map/ppermute | solution.py:58
  583.0 13.4 %slice-start = ((s8[16777216]{0:T(1024)(128)(4,1)}), s8[4194304]{0:T(1024)(128)(4,1)S(1)}, s32[]{:S(2)}) async-start(s8[16777216]{0:T(1024)(128)(4,1)} %bitcast.582), calls=%async_computation.1 | async-start | bytes 8388608
  583.1 13.4 %slice-start.1 = ((s8[16777216]{0:T(1024)(128)(4,1)}), s8[4194304]{0:T(1024)(128)(4,1)S(1)}, s32[]{:S(2)}) async-start(s8[16777216]{0:T(1024)(128)(4,1)} %bitcast.582), calls=%async_computation.2 | async-start | bytes 8388608
  600.6 12.2 %slice-start.60 = ((s8[16777216]{0:T(1024)(128)(4,1)}), s8[4194304]{0:T(1024)(128)(4,1)S(1)}, s32[]{:S(2)}) async-start(s8[16777216]{0:T(1024)(128)(4,1)} %bitcast.632), calls=%async_computation.61 | async-start | bytes 8388608
  600.6 12.2 %slice-start.61 = ((s8[16777216]{0:T(1024)(128)(4,1)}), s8[4194304]{0:T(1024)(128)(4,1)S(1)}, s32[]{:S(2)}) async-start(s8[16777216]{0:T(1024)(128)(4,1)} %bitcast.632), calls=%async_computation.62 | async-start | bytes 8388608
  617.0 14.4 %slice-start.56 = ((s8[16777216]{0:T(1024)(128)(4,1)}), s8[4194304]{0:T(1024)(128)(4,1)S(1)}, s32[]{:S(2)}) async-start(s8[16777216]{0:T(1024)(128)(4,1)} %bitcast.630), calls=%async_computation.57 | async-start | bytes 8388608
  617.0 14.4 %slice-start.57 = ((s8[16777216]{0:T(1024)(128)(4,1)}), s8[4194304]{0:T(1024)(128)(4,1)S(1)}, s32[]{:S(2)}) async-start(s8[16777216]{0:T(1024)(128)(4,1)} %bitcast.630), calls=%async_computation.58 | async-start | bytes 8388608
  639.6 11.9 %slice-start.52 = ((s8[16777216]{0:T(1024)(128)(4,1)}), s8[4194304]{0:T(1024)(128)(4,1)S(1)}, s32[]{:S(2)}) async-start(s8[16777216]{0:T(1024)(128)(4,1)} %bitcast.628), calls=%async_computation.53 | async-start | bytes 8388608
  639.7 11.9 %slice-start.53 = ((s8[16777216]{0:T(1024)(128)(4,1)}), s8[4194304]{0:T(1024)(128)(4,1)S(1)}, s32[]{:S(2)}) async-start(s8[16777216]{0:T(1024)(128)(4,1)} %bitcast.628), calls=%async_computation.54 | async-start | bytes 8388608
  660.0 14.2 %slice-start.48 = ((s8[16777216]{0:T(1024)(128)(4,1)}), s8[4194304]{0:T(1024)(128)(4,1)S(1)}, s32[]{:S(2)}) async-start(s8[16777216]{0:T(1024)(128)(4,1)} %bitcast.626), calls=%async_computation.49 | async-start | bytes 8388608
  660.0 14.2 %slice-start.49 = ((s8[16777216]{0:T(1024)(128)(4,1)}), s8[4194304]{0:T(1024)(128)(4,1)S(1)}, s32[]{:S(2)}) async-start(s8[16777216]{0:T(1024)(128)(4,1)} %bitcast.626), calls=%async_computation.50 | async-start | bytes 8388608
  682.5 12.2 %slice-start.44 = ((s8[16777216]{0:T(1024)(128)(4,1)}), s8[4194304]{0:T(1024)(128)(4,1)S(1)}, s32[]{:S(2)}) async-start(s8[16777216]{0:T(1024)(128)(4,1)} %bitcast.624), calls=%async_computation.45 | async-start | bytes 8388608
  682.5 12.2 %slice-start.45 = ((s8[16777216]{0:T(1024)(128)(4,1)}), s8[4194304]{0:T(1024)(128)(4,1)S(1)}, s32[]{:S(2)}) async-start(s8[16777216]{0:T(1024)(128)(4,1)} %bitcast.624), calls=%async_computation.46 | async-start | bytes 8388608
  703.0 14.2 %slice-start.40 = ((s8[16777216]{0:T(1024)(128)(4,1)}), s8[4194304]{0:T(1024)(128)(4,1)S(1)}, s32[]{:S(2)}) async-start(s8[16777216]{0:T(1024)(128)(4,1)} %bitcast.622), calls=%async_computation.41 | async-start | bytes 8388608
  703.0 14.2 %slice-start.41 = ((s8[16777216]{0:T(1024)(128)(4,1)}), s8[4194304]{0:T(1024)(128)(4,1)S(1)}, s32[]{:S(2)}) async-start(s8[16777216]{0:T(1024)(128)(4,1)} %bitcast.622), calls=%async_computation.42 | async-start | bytes 8388608
  745.7 14.4 %slice-start.32 = ((s8[16777216]{0:T(1024)(128)(4,1)}), s8[4194304]{0:T(1024)(128)(4,1)S(1)}, s32[]{:S(2)}) async-start(s8[16777216]{0:T(1024)(128)(4,1)} %bitcast.618), calls=%async_computation.33 | async-start | bytes 8388608
  745.7 14.4 %slice-start.33 = ((s8[16777216]{0:T(1024)(128)(4,1)}), s8[4194304]{0:T(1024)(128)(4,1)S(1)}, s32[]{:S(2)}) async-start(s8[16777216]{0:T(1024)(128)(4,1)} %bitcast.618), calls=%async_computation.34 | async-start | bytes 8388608
  788.9 14.2 %slice-start.24 = ((s8[16777216]{0:T(1024)(128)(4,1)}), s8[4194304]{0:T(1024)(128)(4,1)S(1)}, s32[]{:S(2)}) async-start(s8[16777216]{0:T(1024)(128)(4,1)} %bitcast.614), calls=%async_computation.25 | async-start | bytes 8388608
  788.9 14.2 %slice-start.25 = ((s8[16777216]{0:T(1024)(128)(4,1)}), s8[4194304]{0:T(1024)(128)(4,1)S(1)}, s32[]{:S(2)}) async-start(s8[16777216]{0:T(1024)(128)(4,1)} %bitcast.614), calls=%async_computation.26 | async-start | bytes 8388608
  811.4 12.0 %slice-start.4 = ((s8[16777216]{0:T(1024)(128)(4,1)}), s8[4194304]{0:T(1024)(128)(4,1)S(1)}, s32[]{:S(2)}) async-start(s8[16777216]{0:T(1024)(128)(4,1)} %bitcast.604), calls=%async_computation.5 | async-start | bytes 8388608
  811.4 12.0 %slice-start.5 = ((s8[16777216]{0:T(1024)(128)(4,1)}), s8[4194304]{0:T(1024)(128)(4,1)S(1)}, s32[]{:S(2)}) async-start(s8[16777216]{0:T(1024)(128)(4,1)} %bitcast.604), calls=%async_computation.6 | async-start | bytes 8388608
  835.8 12.5 %slice-start.8 = ((s8[16777216]{0:T(1024)(128)(4,1)}), s8[4194304]{0:T(1024)(128)(4,1)S(1)}, s32[]{:S(2)}) async-start(s8[16777216]{0:T(1024)(128)(4,1)} %bitcast.606), calls=%async_computation.9 | async-start | bytes 8388608
  835.8 12.5 %slice-start.9 = ((s8[16777216]{0:T(1024)(128)(4,1)}), s8[4194304]{0:T(1024)(128)(4,1)S(1)}, s32[]{:S(2)}) async-start(s8[16777216]{0:T(1024)(128)(4,1)} %bitcast.606), calls=%async_computation.10 | async-start | bytes 8388608
  856.6 12.3 %slice-start.12 = ((s8[16777216]{0:T(1024)(128)(4,1)}), s8[4194304]{0:T(1024)(128)(4,1)S(1)}, s32[]{:S(2)}) async-start(s8[16777216]{0:T(1024)(128)(4,1)} %bitcast.608), calls=%async_computation.13 | async-start | bytes 8388608
  856.6 12.3 %slice-start.13 = ((s8[16777216]{0:T(1024)(128)(4,1)}), s8[4194304]{0:T(1024)(128)(4,1)S(1)}, s32[]{:S(2)}) async-start(s8[16777216]{0:T(1024)(128)(4,1)} %bitcast.608), calls=%async_computation.14 | async-start | bytes 8388608
  877.6 12.3 %slice-start.16 = ((s8[16777216]{0:T(1024)(128)(4,1)}), s8[4194304]{0:T(1024)(128)(4,1)S(1)}, s32[]{:S(2)}) async-start(s8[16777216]{0:T(1024)(128)(4,1)} %bitcast.610), calls=%async_computation.17 | async-start | bytes 8388608
  877.6 12.3 %slice-start.17 = ((s8[16777216]{0:T(1024)(128)(4,1)}), s8[4194304]{0:T(1024)(128)(4,1)S(1)}, s32[]{:S(2)}) async-start(s8[16777216]{0:T(1024)(128)(4,1)} %bitcast.610), calls=%async_computation.18 | async-start | bytes 8388608
  898.1 12.4 %slice-start.20 = ((s8[16777216]{0:T(1024)(128)(4,1)}), s8[4194304]{0:T(1024)(128)(4,1)S(1)}, s32[]{:S(2)}) async-start(s8[16777216]{0:T(1024)(128)(4,1)} %bitcast.612), calls=%async_computation.21 | async-start | bytes 8388608
  898.2 12.4 %slice-start.21 = ((s8[16777216]{0:T(1024)(128)(4,1)}), s8[4194304]{0:T(1024)(128)(4,1)S(1)}, s32[]{:S(2)}) async-start(s8[16777216]{0:T(1024)(128)(4,1)} %bitcast.612), calls=%async_computation.22 | async-start | bytes 8388608
  (37 other events, 295.4 us)
Sparse Core Ops, SparseCore 0:
  18.7 564.2 all-gather.1
